TPU v7x, 128 devices: a whole 4x4x4 slice. The times are simulated.
128 devices in a mesh: group: 4 (over x), bulk: 32 (over z, y, core).
Axes of the slice: x: 4, y: 4, z: 4, core: 2. Of those that a mesh axis runs over, the one named last changes fastest.
Arguments:
- rhs: float32 [512, 64, 128], P(('group', 'bulk')), may hold values from -90 to 90, as said below
- diag_tiles: float32 [512, 128, 128], P(('group', 'bulk')), may hold values from -0.06 to 0.06
- offdiag_blocks: float32 [512, 11, 128, 128], P(('group', 'bulk')), may hold values from -0.026 to 0.026
- coupling: float32 [256, 4, 128, 128], P(('group', 'bulk')), may hold values from -0.05 to 0.05, as said below
- col_index: int32 [512, 11], replicated, may hold values from 0 to 511, as said below
- load: int32 [512], replicated, may hold values from 3 to 11
- new_slot: int32 [512], replicated, may hold values from 0 to 511, as said below
Outputs:
- solution_out: float32 [512, 64, 128], P(('group', 'bulk'))
- residual_out: float32 [512, 64, 128], P(('group', 'bulk'))
Inputs may be any that keep to these rules, and one draw needn't show every extreme that they name: `rhs`: made of random entries times scales of the rows and of the columns. `coupling`: entry [d * 2 + k, h] is the transpose of entry [(h * 32 + d % 32) * 2 + k, d // 32]. `col_index`: for each part g and each tile position t, the column t of the 128 block rows of part g is a permutation of that part's slots g * 128 to (g + 1) * 128 - 1. Of the 44 entries of the 4 block rows of one device (slots d * 4 to (d + 1) * 4 - 1), at most 2 name slots of any one device, and exactly 2 name slots of some device. `new_slot`: A permutation. On every device exactly one block row moves, from a slot k with 2 <= k % 4; it stays in its part, goes from owner b to owner b XOR m, where m (1 to 31) is one number for the whole part, and takes the slot that the moving row of that device leaves.
All inputs are finite; a program needn't handle non-finite values.
Results may differ from a plain program's by a relative error of at most 0.0003.
Values sent between devices are 32-bit elements; how exact they have to be, the bound alone decides.
A program may use at most 64 MiB of HBM per device.

v0:
```python
import jax
import jax.numpy as jnp
from jax import lax
from jax.sharding import PartitionSpec as P

highest = lax.Precision.HIGHEST
diagonal_shift = 4.0


def from_partner(value, axis, bit):
    mask = 2**bit
    pairs = [(source, source ^ mask) for source in range(lax.axis_size(axis))]
    return lax.ppermute(value, axis, pairs)


def chol_apply(matrix, right):
    factor = jnp.linalg.cholesky(matrix)
    middle = lax.linalg.triangular_solve(factor, right, left_side=True, lower=True)
    return lax.linalg.triangular_solve(factor, middle, left_side=True, lower=True, transpose_a=True)


def global_gram(left, right):
    partial_gram = jnp.einsum("snt,smt->nm", left, right, precision=highest)
    total = lax.psum(partial_gram, ("group", "bulk"))
    return 0.5 * (total + total.T)


def operate(vectors, diag, masked, column_ids, coupling):
    row_count = vectors.shape[0]
    boundary_rows = coupling.shape[0]
    part_count = coupling.shape[1]
    group_rows = row_count * lax.axis_size("bulk")
    border = lax.all_gather(vectors[:boundary_rows], "group", axis=0, tiled=True)
    final_output = diagonal_shift * vectors + jnp.einsum(
        "rnj,rij->rni", vectors, diag, precision=highest
    )
    returned = jnp.einsum("rni,rkij->rknj", vectors, masked, precision=highest)
    flat_terms = returned.reshape((-1,) + vectors.shape[1:])
    panel = lax.all_gather(vectors, "bulk", axis=0, tiled=True)
    buffer = jax.ops.segment_sum(flat_terms, column_ids.reshape(-1), num_segments=group_rows)
    owed = lax.psum_scatter(buffer, "bulk", scatter_dimension=0, tiled=True)
    picked = panel[column_ids]
    final_output = (
        final_output + jnp.einsum("rknj,rkij->rni", picked, masked, precision=highest) + owed
    )
    border = border.reshape((part_count, boundary_rows) + vectors.shape[1:])
    crossed = jnp.einsum("khij,hknj->kni", coupling, border, precision=highest)
    return final_output.at[:boundary_rows].add(crossed)


def advance(state, diag, masked, column_ids, coupling, last_step):
    solution, resid, direction, gram_rr = state
    image = operate(direction, diag, masked, column_ids, coupling)
    gram_pq = global_gram(direction, image)
    alpha = chol_apply(gram_pq, gram_rr)
    solution = solution + jnp.einsum("mn,smt->snt", alpha, direction, precision=highest)
    resid = resid - jnp.einsum("mn,smt->snt", alpha, image, precision=highest)
    if not last_step:
        gram_new = global_gram(resid, resid)
        beta = chol_apply(gram_rr, gram_new)
        direction = resid + jnp.einsum("mn,smt->snt", beta, direction, precision=highest)
        gram_rr = gram_new
    return (solution, resid, direction, gram_rr)


def local(rhs, diag_tiles, offdiag_blocks, coupling, col_index, load, new_slot):
    row_count = rhs.shape[0]
    off_count = offdiag_blocks.shape[1]
    bulk_count = lax.axis_size("bulk")
    group_rows = row_count * bulk_count
    my_group = lax.axis_index("group")
    my_bulk = lax.axis_index("bulk")
    first_slot = (my_group * bulk_count + my_bulk) * row_count
    group_base = my_group * group_rows
    own_slots = first_slot + jnp.arange(row_count, dtype=jnp.int32)
    tile_ids = jnp.arange(off_count, dtype=jnp.int32)
    old_columns = col_index[own_slots] - group_base
    old_mask = (tile_ids[None, :] < load[own_slots][:, None]).astype(jnp.float32)
    old_masked = offdiag_blocks * old_mask[:, :, None, None]
    own_new = new_slot[own_slots]
    leaving = jnp.argmax((own_new != own_slots).astype(jnp.int32))
    target = own_new[leaving]
    target_bulk = target // row_count % bulk_count
    xor_mask = jnp.bitwise_xor(target_bulk, my_bulk)
    start_state = (jnp.zeros_like(rhs), rhs, rhs, global_gram(rhs, rhs))
    state = advance(start_state, diag_tiles, old_masked, old_columns, coupling, False)
    solution, resid, direction, gram_rr = state
    pieces = [
        offdiag_blocks[leaving],
        diag_tiles[leaving],
        solution[leaving],
        resid[leaving],
        direction[leaving],
    ]
    flat = jnp.concatenate([piece.reshape(-1) for piece in pieces])
    for bit_pos in range(bulk_count.bit_length() - 1):
        partner = from_partner(flat, "bulk", bit_pos)
        chosen = jnp.bitwise_and(jnp.right_shift(xor_mask, bit_pos), 1) == 1
        flat = jnp.where(chosen, partner, flat)
    outputs = []
    offset = 0
    for piece in pieces:
        outputs.append(flat[offset : offset + piece.size].reshape(piece.shape))
        offset = offset + piece.size
    moved_off = offdiag_blocks.at[leaving].set(outputs[0])
    moved_diag = diag_tiles.at[leaving].set(outputs[1])
    solution = solution.at[leaving].set(outputs[2])
    resid = resid.at[leaving].set(outputs[3])
    direction = direction.at[leaving].set(outputs[4])
    inverse = (
        jnp.zeros_like(new_slot).at[new_slot].set(jnp.arange(new_slot.shape[0], dtype=jnp.int32))
    )
    old_rows = inverse[own_slots]
    new_columns = new_slot[col_index[old_rows]] - group_base
    new_mask = (tile_ids[None, :] < load[old_rows][:, None]).astype(jnp.float32)
    new_masked = moved_off * new_mask[:, :, None, None]
    state = advance(
        (solution, resid, direction, gram_rr), moved_diag, new_masked, new_columns, coupling, True
    )
    return (state[0], state[1])


def solution(mesh):
    return jax.shard_map(
        local,
        mesh=mesh,
        in_specs=(
            P(("group", "bulk"), None, None),
            P(("group", "bulk"), None, None),
            P(("group", "bulk"), None, None, None),
            P(("group", "bulk"), None, None, None),
            P(),
            P(),
            P(),
        ),
        out_specs=(P(("group", "bulk"), None, None), P(("group", "bulk"), None, None)),
        check_vma=False,
    )
```

profile of v0, /device:TPU:1, one launch (start us, length us, event | category | flops | bytes accessed | tf_op | source)
XLA Modules:
  0.0 662.4 jit_solution(1041182074401895514)
XLA Ops:
  31.0 8.0 %scatter_fusion = f32[128,64,128]{2,1,0:T(8,128)} fusion(f32[128,64,128]{2,1,0:T(8,128)} %broadcast.320.clone, s32[44]{0:T(128)} %reshape.516, f32[44,64,128]{2,1,0:T(8,128)} %bitcast.222), kind=kCustom, calls=%fused_computation.9 | custom fusion | flops 360448 | bytes 4325552 | tf_op jit(solution)/shard_map/scatter-add | solution.py:40
  45.5 13.0 %all_gather.13 = f32[8,64,128]{2,1,0:T(8,128)} all-gather(f32[2,64,128]{2,1,0:T(8,128)} %slice.208), channel_id=1, replica_groups=mesh['group'=4,'bulk'=32] {'group'}, dimensions={0}, use_global_device_ids=true | all-gather | bytes 327680 | tf_op jit(solution)/shard_map/all_gather | solution.py:33
  62.4 4.0 gather_fusion.1
  66.4 5.4 fusion.12
  71.8 71.6 %reduce-scatter.3.cloned.1.call-done = f32[4,64,128]{2,1,0:T(8,128)} async-done(((f32[128,64,128]{2,1,0:T(8,128)}), f32[4,64,128]{2,1,0:T(8,128)}) %reduce-scatter.3.cloned.1.call-update) | async-done | bytes 131088 | tf_op jit(solution)/shard_map/reduce_scatter | solution.py:41
  148.2 66.3 %all-reduce = (f32[64,64]{1,0:T(8,128)}, f32[64,64]{1,0:T(8,128)}) all-reduce(f32[64,64]{1,0:T(8,128)} %convolution_bitcast_fusion.11, f32[64,64]{1,0:T(8,128)} %convolution_bitcast_fusion.12), channel_id=1, replica_groups=mesh['group'=4,'bulk'=32] {'group','bulk'}, use_global_device_ids=true, to_apply=%region_5.7 | all-reduce | flops 8192 | bytes 65536 | tf_op jit(solution)/shard_map/psum | solution.py:24
  224.5 7.2 %cholesky.59 = f32[64,64]{1,0:T(8,128)} custom-call(f32[64,64]{1,0:T(8,128)} %fusion.60), custom_call_target="Cholesky" | custom-call | tf_op jit(solution)/shard_map/jit(cholesky)/cholesky | solution.py:17
  235.3 6.3 custom-call.13
  247.7 7.2 %cholesky.70 = f32[64,64]{1,0:T(8,128)} custom-call(f32[64,64]{1,0:T(8,128)} %fusion.55), custom_call_target="Cholesky" | custom-call | tf_op jit(solution)/shard_map/jit(cholesky)/cholesky | solution.py:17
  258.5 6.3 custom-call.15
  266.6 63.0 %psum.30 = f32[64,64]{1,0:T(8,128)} all-reduce(f32[64,64]{1,0:T(8,128)} %convolution_bitcast_fusion.9), channel_id=1, replica_groups=mesh['group'=4,'bulk'=32] {'group','bulk'}, use_global_device_ids=true, to_apply=%region_8.12 | all-reduce | flops 4096 | bytes 32768 | tf_op jit(solution)/shard_map/psum | solution.py:24
  344.7 20.3 %collective-permute-done.1 = f32[221184]{0:T(1024)} collective-permute-done((f32[221184]{0:T(1024)}, f32[221184]{0:T(1024)}, u32[]{:S(2)}, u32[]{:S(2)}) %collective-permute-start.1) | collective-permute-done | bytes 884768 | tf_op jit(solution)/shard_map/ppermute | solution.py:13
  370.2 19.2 %collective-permute-done.2 = f32[221184]{0:T(1024)} collective-permute-done((f32[221184]{0:T(1024)}, f32[221184]{0:T(1024)}, u32[]{:S(2)}, u32[]{:S(2)}) %collective-permute-start.2) | collective-permute-done | bytes 884768 | tf_op jit(solution)/shard_map/ppermute | solution.py:13
  392.7 18.7 %collective-permute-done.3 = f32[221184]{0:T(1024)} collective-permute-done((f32[221184]{0:T(1024)}, f32[221184]{0:T(1024)}, u32[]{:S(2)}, u32[]{:S(2)}) %collective-permute-start.3) | collective-permute-done | bytes 884768 | tf_op jit(solution)/shard_map/ppermute | solution.py:13
  416.7 17.4 %collective-permute-done.4 = f32[221184]{0:T(1024)} collective-permute-done((f32[221184]{0:T(1024)}, f32[221184]{0:T(1024)}, u32[]{:S(2)}, u32[]{:S(2)}) %collective-permute-start.4) | collective-permute-done | bytes 884768 | tf_op jit(solution)/shard_map/ppermute | solution.py:13
  451.1 7.8 %scatter_fusion.1 = f32[128,64,128]{2,1,0:T(8,128)} fusion(f32[128,64,128]{2,1,0:T(8,128)} %broadcast.320, s32[44]{0:T(128)S(1)} %broadcast_subtract_fusion.1, f32[44,64,128]{2,1,0:T(8,128)} %bitcast.223), kind=kCustom, calls=%fused_computation.11 | custom fusion | flops 360448 | bytes 4325552 | tf_op jit(solution)/shard_map/scatter-add | solution.py:40
  459.2 10.1 %all_gather.15 = f32[8,64,128]{2,1,0:T(8,128)} all-gather(f32[2,64,128]{2,1,0:T(8,128)S(1)} %slice.243), channel_id=1, replica_groups=mesh['group'=4,'bulk'=32] {'group'}, dimensions={0}, use_global_device_ids=true | all-gather | bytes 327680 | tf_op jit(solution)/shard_map/all_gather | solution.py:33
  471.4 15.3 %all-gather.5.cloned.1.call-done = f32[128,64,128]{2,1,0:T(8,128)} async-done(((f32[4,64,128]{2,1,0:T(8,128)}), f32[128,64,128]{2,1,0:T(8,128)}) %all-gather.5.cloned.1.call-update) | async-done | bytes 4194320 | tf_op jit(solution)/shard_map/all_gather | solution.py:39
  486.7 4.0 gather_fusion.7
  490.7 5.4 fusion.15
  496.2 73.8 %reduce-scatter.5.cloned.1.call-done = f32[4,64,128]{2,1,0:T(8,128)} async-done(((f32[128,64,128]{2,1,0:T(8,128)}), f32[4,64,128]{2,1,0:T(8,128)}) %reduce-scatter.5.cloned.1.call-update) | async-done | bytes 131088 | tf_op jit(solution)/shard_map/reduce_scatter | solution.py:41
  573.5 66.0 %psum.31 = f32[64,64]{1,0:T(8,128)S(1)} all-reduce(f32[64,64]{1,0:T(8,128)S(1)} %convolution_bitcast_fusion.7), channel_id=1, replica_groups=mesh['group'=4,'bulk'=32] {'group','bulk'}, use_global_device_ids=true, to_apply=%region_13.17 | all-reduce | flops 4096 | bytes 32768 | tf_op jit(solution)/shard_map/psum | solution.py:24
  639.7 5.8 cholesky.81
  646.9 4.9 custom-call.17
  (142 shorter events, 116.7 us)
Async XLA Ops:
  7.2 137.9 %copy-start = (f32[2,4,128,128]{3,2,1,0:T(8,128)S(1)}, f32[2,4,128,128]{3,2,1,0:T(8,128)}, u32[]{:S(2)}) copy-start(f32[2,4,128,128]{3,2,1,0:T(8,128)} %param.29) | copy-start | bytes 1572868
  7.2 18.1 %copy-start.3 = (f32[4,64,128]{2,1,0:T(8,128)S(1)}, f32[4,64,128]{2,1,0:T(8,128)}, u32[]{:S(2)}) copy-start(f32[4,64,128]{2,1,0:T(8,128)} %param.26) | copy-start | bytes 393220
  7.2 16.2 %copy-start.2 = (s32[512]{0:T(512)S(1)}, s32[512]{0:T(512)}, u32[]{:S(2)}) copy-start(s32[512]{0:T(512)} %param.31) | copy-start | bytes 6148
  7.2 4.3 copy-start.1
  7.2 55.2 %all-gather.3.cloned.1.call-start = ((), (), s32[]{:S(2)}) async-start(), calls=%async_computation.2 | async-start | bytes 4325376 | tf_op jit(solution)/shard_map/all_gather | solution.py:39
  7.3 1.9 copy-start.11
  9.9 133.5 %reduce-scatter.3.cloned.1.call-start = ((), (), s32[]{:S(2)}) async-start(), calls=%async_computation.3 | async-start | bytes 4325376 | tf_op jit(solution)/shard_map/reduce_scatter | solution.py:41
  39.0 447.7 %all-gather.5.cloned.1.call-start = ((), (), s32[]{:S(2)}) async-start(), calls=%async_computation.4 | async-start | bytes 4325376 | tf_op jit(solution)/shard_map/all_gather | solution.py:39
  71.8 266.4 %copy-start.13 = (s32[4]{0:T(128)S(1)}, s32[4]{0:T(128)}, u32[]{:S(2)}) copy-start(s32[4]{0:T(128)} %gather_fusion.3) | copy-start | bytes 52
  146.7 0.7 copy-start.7
  334.2 2.8 copy-start.4
  337.6 3.7 collective-permute-start
  343.5 21.5 %collective-permute-start.1 = (f32[221184]{0:T(1024)}, f32[221184]{0:T(1024)}, u32[]{:S(2)}, u32[]{:S(2)}) collective-permute-start(f32[221184]{0:T(1024)} %broadcast_select_fusion), channel_id=1, source_target_pairs={{0,2},{1,3},{2,0},{3,1},{4,6},{5,7},{6,4},{7,5},{8,10},{9,11},{10,... | collective-permute-start | bytes 2654216 | tf_op jit(solution)/shard_map/ppermute | solution.py:13
  367.2 48.7 %copy-start.14 = (s32[3]{0:T(128)S(1)}, s32[3]{0:T(128)}, u32[]{:S(2)}) copy-start(s32[3]{0:T(128)} %constant.237.clone.1) | copy-start | bytes 40
  367.2 49.5 %copy-start.8 = (f32[64,4,128]{2,0,1:T(8,128)S(1)}, f32[64,4,128]{2,0,1:T(8,128)}, u32[]{:S(2)}) copy-start(f32[64,4,128]{2,0,1:T(8,128)} %fusion.73) | copy-start | bytes 393220
  367.2 22.2 %collective-permute-start.2 = (f32[221184]{0:T(1024)}, f32[221184]{0:T(1024)}, u32[]{:S(2)}, u32[]{:S(2)}) collective-permute-start(f32[221184]{0:T(1024)} %broadcast_select_fusion.1), channel_id=1, source_target_pairs={{0,4},{1,5},{2,6},{3,7},{4,0},{5,1},{6,2},{7,3},{8,12},{9,13},{10,... | collective-permute-start | bytes 2654216 | tf_op jit(solution)/shard_map/ppermute | solution.py:13
  391.6 19.8 %collective-permute-start.3 = (f32[221184]{0:T(1024)}, f32[221184]{0:T(1024)}, u32[]{:S(2)}, u32[]{:S(2)}) collective-permute-start(f32[221184]{0:T(1024)} %broadcast_select_fusion.2), channel_id=1, source_target_pairs={{0,8},{1,9},{2,10},{3,11},{4,12},{5,13},{6,14},{7,15},{8,0},{9,1},... | collective-permute-start | bytes 2654216 | tf_op jit(solution)/shard_map/ppermute | solution.py:13
  392.7 47.8 %copy-start.12 = (s32[4,11,1]{1,0,2:T(4,128)S(1)}, s32[4,11,1]{1,0,2:T(4,128)}, u32[]{:S(2)}) copy-start(s32[4,11,1]{1,0,2:T(4,128)} %get-tuple-element.98) | copy-start | bytes 532
  413.6 20.5 %collective-permute-start.4 = (f32[221184]{0:T(1024)}, f32[221184]{0:T(1024)}, u32[]{:S(2)}, u32[]{:S(2)}) collective-permute-start(f32[221184]{0:T(1024)} %broadcast_select_fusion.3), channel_id=1, source_target_pairs={{0,16},{1,17},{2,18},{3,19},{4,20},{5,21},{6,22},{7,23},{8,24},{9,... | collective-permute-start | bytes 2654216 | tf_op jit(solution)/shard_map/ppermute | solution.py:13
  435.3 0.9 copy-start.6
  438.3 0.7 copy-start.9
  438.9 131.0 %reduce-scatter.5.cloned.1.call-start = ((), (), s32[]{:S(2)}) async-start(), calls=%async_computation.5 | async-start | bytes 4325376 | tf_op jit(solution)/shard_map/reduce_scatter | solution.py:41
  440.5 4.9 copy-start.5
  496.2 158.8 %copy-start.10 = (f32[4,64,128]{2,1,0:T(8,128)S(1)}, f32[4,64,128]{2,1,0:T(8,128)}, u32[]{:S(2)}) copy-start(f32[4,64,128]{2,1,0:T(8,128)} %copy-done.9) | copy-start | bytes 393220
Sparse Core Ops, SparseCore 0:
  10.3 49.7 all-gather.2
  63.7 79.6 reduce-scatter.2
  439.1 47.6 all-gather.4
  490.2 79.7 reduce-scatter.4
where the time goes:
time: 666 us; the launch traced here: 662 us
  waiting for transfers between devices  236 us (35%)
  blocking collectives  218 us (33%)
  other arithmetic  90.6 us (14%)
  local copies, waits for them, and re-layouts  50.3 us (8%)
  matrix products  39.5 us (6%)
  between operations  18.6 us (3%)
  starting transfers between devices  8.54 us (1%)
    psum x3, blocking collectives, global_gram(): total = lax.psum(partial_gram, ('group', 'bulk'))  195 us
    reduce_scatter x2, waiting for transfers between devices, operate(): owed = lax.psum_scatter(buffer, 'bulk', scatter_dimension=0, tiled=True)  145 us
    ppermute x5, waiting for transfers between devices, from_partner(): return lax.ppermute(value, axis, pairs)  75.6 us
    another operation x9, other arithmetic, chol_apply(): factor = jnp.linalg.cholesky(matrix)  23.9 us
    all_gather x2, blocking collectives, operate(): lax.all_gather(vectors[:boundary_rows], 'group', axis=0, tiled=True)  23.1 us
    another operation x6, other arithmetic, chol_apply(): lax.linalg.triangular_solve(factor, middle, left_side=True, lower=True, t...  22.2 us
    scatter-add x2, other arithmetic, operate(): jax.ops.segment_sum(flat_terms, column_ids.reshape(-1), num_segments=grou...  15.8 us
    all_gather x2, waiting for transfers between devices, operate(): panel = lax.all_gather(vectors, 'bulk', axis=0, tiled=True)  15.3 us
  transfers between devices with their start and end apart: 9, of which 7 were waited for; matrix products, arithmetic and copies ran while one was open for 12% of the time, Pallas kernels for 0%

commit v1 on v0

--- a/solution.py
+++ b/solution.py
@@ -2,6 +2,7 @@
 import jax.numpy as jnp
 from jax import lax
 from jax.sharding import PartitionSpec as P
+from jax.lax import psum
 
 highest = lax.Precision.HIGHEST
 diagonal_shift = 4.0
@@ -21,7 +22,7 @@
 
 def global_gram(left, right):
     partial_gram = jnp.einsum("snt,smt->nm", left, right, precision=highest)
-    total = lax.psum(partial_gram, ("group", "bulk"))
+    total = psum(psum(partial_gram, axis_name="bulk"), axis_name="group")
     return 0.5 * (total + total.T)
 
 

time: 666 us -> 894 us (1.34)
  blocking collectives: 218 us -> 434 us
    psum x3 -> x6, blocking collectives: 195 us -> 410 us  [global_gram(): total = psum(psum(partial_gram, axis_name='bulk'), axis_name='group')]
  transfers between devices with their start and end apart: 9 -> 9, of which waited for: 7 -> 7; matrix products, arithmetic and copies ran while one was open for 12% -> 9% of each run, Pallas kernels for 0% -> 0%
where the time goes in v1:
time: 894 us; the launch traced here: 883 us
  blocking collectives  434 us (49%)
  waiting for transfers between devices  241 us (27%)
  other arithmetic  90.6 us (10%)
  local copies, waits for them, and re-layouts  50.3 us (6%)
  matrix products  38.6 us (4%)
  between operations  18.6 us (2%)
  starting transfers between devices  9.3 us (1%)
    psum x6, blocking collectives, global_gram(): total = psum(psum(partial_gram, axis_name='bulk'), axis_name='group')  410 us
    reduce_scatter x2, waiting for transfers between devices, operate(): owed = lax.psum_scatter(buffer, 'bulk', scatter_dimension=0, tiled=True)  145 us
    ppermute x5, waiting for transfers between devices, from_partner(): return lax.ppermute(value, axis, pairs)  83.1 us
    another operation x9, other arithmetic, chol_apply(): factor = jnp.linalg.cholesky(matrix)  23.9 us
    all_gather x2, blocking collectives, operate(): lax.all_gather(vectors[:boundary_rows], 'group', axis=0, tiled=True)  23.3 us
    another operation x6, other arithmetic, chol_apply(): lax.linalg.triangular_solve(factor, middle, left_side=True, lower=True, t...  22.2 us
  transfers between devices with their start and end apart: 9, of which 7 were waited for; matrix products, arithmetic and copies ran while one was open for 9% of the time, Pallas kernels for 0%

profile of v1, /device:TPU:1, one launch (start us, length us, event | category | flops | bytes accessed | tf_op | source)
XLA Modules:
  0.0 882.6 jit_solution(7572151993584937753)
XLA Ops:
  31.0 8.0 scatter_fusion
  45.5 13.0 %all_gather.13 = f32[8,64,128]{2,1,0:T(8,128)} all-gather(f32[2,64,128]{2,1,0:T(8,128)} %slice.208), channel_id=1, replica_groups=mesh['group'=4,'bulk'=32] {'group'}, dimensions={0}, use_global_device_ids=true | all-gather | bytes 327680 | tf_op jit(solution)/shard_map/all_gather | solution.py:34
  66.4 5.4 fusion.12
  71.8 71.6 %reduce-scatter.3.cloned.1.call-done = f32[4,64,128]{2,1,0:T(8,128)} async-done(((f32[128,64,128]{2,1,0:T(8,128)}), f32[4,64,128]{2,1,0:T(8,128)}) %reduce-scatter.3.cloned.1.call-update) | async-done | bytes 131088 | tf_op jit(solution)/shard_map/reduce_scatter | solution.py:42
  148.2 121.1 %all-reduce = (f32[64,64]{1,0:T(8,128)}, f32[64,64]{1,0:T(8,128)}) all-reduce(f32[64,64]{1,0:T(8,128)} %convolution_bitcast_fusion.11, f32[64,64]{1,0:T(8,128)} %convolution_bitcast_fusion.12), channel_id=1, replica_groups=mesh['group'=4,'bulk'=32] {'bulk'}, use_global_device_ids=true, to_apply=%region_6.8 | all-reduce | flops 8192 | bytes 65536 | tf_op jit(solution)/shard_map/psum | solution.py:25
  269.3 14.8 %all-reduce.1 = (f32[64,64]{1,0:T(8,128)}, f32[64,64]{1,0:T(8,128)}) all-reduce(f32[64,64]{1,0:T(8,128)} %get-tuple-element.91, f32[64,64]{1,0:T(8,128)} %get-tuple-element.92), channel_id=1, replica_groups=mesh['group'=4,'bulk'=32] {'group'}, use_global_device_ids=true, to_apply=%region_7.9 | all-reduce | flops 8192 | bytes 65536 | tf_op jit(solution)/shard_map/psum | solution.py:25
  294.0 7.2 cholesky.59
  304.8 6.3 custom-call.13
  317.2 7.2 cholesky.70
  328.0 6.3 custom-call.15
  336.1 128.1 %psum.60 = f32[64,64]{1,0:T(8,128)} all-reduce(f32[64,64]{1,0:T(8,128)} %convolution_bitcast_fusion.9), channel_id=1, replica_groups=mesh['group'=4,'bulk'=32] {'bulk'}, use_global_device_ids=true, to_apply=%region_10.14 | all-reduce | flops 4096 | bytes 32768 | tf_op jit(solution)/shard_map/psum | solution.py:25
  464.2 12.1 %psum.61 = f32[64,64]{1,0:T(8,128)} all-reduce(f32[64,64]{1,0:T(8,128)} %psum.60), channel_id=1, replica_groups=mesh['group'=4,'bulk'=32] {'group'}, use_global_device_ids=true, to_apply=%region_11.15 | all-reduce | flops 4096 | bytes 32768 | tf_op jit(solution)/shard_map/psum | solution.py:25
  484.3 9.1 %collective-permute-start = (f32[221184]{0:T(1024)}, f32[221184]{0:T(1024)}, u32[]{:S(2)}, u32[]{:S(2)}) collective-permute-start(f32[221184]{0:T(1024)} %bitcast_dynamic-update-slice_fusion.1), channel_id=1, source_target_pairs={{0,1},{1,0},{2,3},{3,2},{4,5},{5,4},{6,7},{7,6},{8,9},{9,8},{10,11... | collective-permute-start | bytes 2654216 | tf_op jit(solution)/shard_map/ppermute | solution.py:14
  498.7 21.5 %collective-permute-done.1 = f32[221184]{0:T(1024)} collective-permute-done((f32[221184]{0:T(1024)}, f32[221184]{0:T(1024)}, u32[]{:S(2)}, u32[]{:S(2)}) %collective-permute-start.1) | collective-permute-done | bytes 884768 | tf_op jit(solution)/shard_map/ppermute | solution.py:14
  522.5 22.2 %collective-permute-done.2 = f32[221184]{0:T(1024)} collective-permute-done((f32[221184]{0:T(1024)}, f32[221184]{0:T(1024)}, u32[]{:S(2)}, u32[]{:S(2)}) %collective-permute-start.2) | collective-permute-done | bytes 884768 | tf_op jit(solution)/shard_map/ppermute | solution.py:14
  546.9 19.8 %collective-permute-done.3 = f32[221184]{0:T(1024)} collective-permute-done((f32[221184]{0:T(1024)}, f32[221184]{0:T(1024)}, u32[]{:S(2)}, u32[]{:S(2)}) %collective-permute-start.3) | collective-permute-done | bytes 884768 | tf_op jit(solution)/shard_map/ppermute | solution.py:14
  569.6 19.7 %collective-permute-done.4 = f32[221184]{0:T(1024)} collective-permute-done((f32[221184]{0:T(1024)}, f32[221184]{0:T(1024)}, u32[]{:S(2)}, u32[]{:S(2)}) %collective-permute-start.4) | collective-permute-done | bytes 884768 | tf_op jit(solution)/shard_map/ppermute | solution.py:14
  606.1 7.8 scatter_fusion.1
  614.2 10.3 %all_gather.15 = f32[8,64,128]{2,1,0:T(8,128)} all-gather(f32[2,64,128]{2,1,0:T(8,128)S(1)} %slice.243), channel_id=1, replica_groups=mesh['group'=4,'bulk'=32] {'group'}, dimensions={0}, use_global_device_ids=true | all-gather | bytes 327680 | tf_op jit(solution)/shard_map/all_gather | solution.py:34
  626.6 12.9 %all-gather.5.cloned.1.call-done = f32[128,64,128]{2,1,0:T(8,128)} async-done(((f32[4,64,128]{2,1,0:T(8,128)}), f32[128,64,128]{2,1,0:T(8,128)}) %all-gather.5.cloned.1.call-update) | async-done | bytes 4194320 | tf_op jit(solution)/shard_map/all_gather | solution.py:40
  649.0 73.8 %reduce-scatter.5.cloned.1.call-done = f32[4,64,128]{2,1,0:T(8,128)} async-done(((f32[128,64,128]{2,1,0:T(8,128)}), f32[4,64,128]{2,1,0:T(8,128)}) %reduce-scatter.5.cloned.1.call-update) | async-done | bytes 131088 | tf_op jit(solution)/shard_map/reduce_scatter | solution.py:42
  726.3 120.9 %psum.62 = f32[64,64]{1,0:T(8,128)S(1)} all-reduce(f32[64,64]{1,0:T(8,128)S(1)} %convolution_bitcast_fusion.7), channel_id=1, replica_groups=mesh['group'=4,'bulk'=32] {'bulk'}, use_global_device_ids=true, to_apply=%region_16.20 | all-reduce | flops 4096 | bytes 32768 | tf_op jit(solution)/shard_map/psum | solution.py:25
  847.2 13.4 %psum.63 = f32[64,64]{1,0:T(8,128)S(1)} all-reduce(f32[64,64]{1,0:T(8,128)S(1)} %psum.62), channel_id=1, replica_groups=mesh['group'=4,'bulk'=32] {'group'}, use_global_device_ids=true, to_apply=%region_17.21 | all-reduce | flops 4096 | bytes 32768 | tf_op jit(solution)/shard_map/psum | solution.py:25
  860.8 5.8 cholesky.81
  (147 shorter events, 125.8 us)
Async XLA Ops:
  7.2 137.9 %copy-start = (f32[2,4,128,128]{3,2,1,0:T(8,128)S(1)}, f32[2,4,128,128]{3,2,1,0:T(8,128)}, u32[]{:S(2)}) copy-start(f32[2,4,128,128]{3,2,1,0:T(8,128)} %param.29) | copy-start | bytes 1572868
  7.2 18.1 %copy-start.3 = (f32[4,64,128]{2,1,0:T(8,128)S(1)}, f32[4,64,128]{2,1,0:T(8,128)}, u32[]{:S(2)}) copy-start(f32[4,64,128]{2,1,0:T(8,128)} %param.26) | copy-start | bytes 393220
  7.2 16.2 %copy-start.2 = (s32[512]{0:T(512)S(1)}, s32[512]{0:T(512)}, u32[]{:S(2)}) copy-start(s32[512]{0:T(512)} %param.31) | copy-start | bytes 6148
  7.2 4.3 copy-start.1
  7.2 55.2 %all-gather.3.cloned.1.call-start = ((), (), s32[]{:S(2)}) async-start(), calls=%async_computation.2 | async-start | bytes 4325376 | tf_op jit(solution)/shard_map/all_gather | solution.py:40
  7.3 1.9 copy-start.12
  9.9 133.5 %reduce-scatter.3.cloned.1.call-start = ((), (), s32[]{:S(2)}) async-start(), calls=%async_computation.3 | async-start | bytes 4325376 | tf_op jit(solution)/shard_map/reduce_scatter | solution.py:42
  39.0 600.5 %all-gather.5.cloned.1.call-start = ((), (), s32[]{:S(2)}) async-start(), calls=%async_computation.4 | async-start | bytes 4325376 | tf_op jit(solution)/shard_map/all_gather | solution.py:40
  71.8 421.6 %copy-start.14 = (s32[4]{0:T(128)S(1)}, s32[4]{0:T(128)}, u32[]{:S(2)}) copy-start(s32[4]{0:T(128)} %gather_fusion.3) | copy-start | bytes 52
  146.7 0.7 copy-start.8
  480.9 2.8 copy-start.4
  484.3 12.2 %collective-permute-start = (f32[221184]{0:T(1024)}, f32[221184]{0:T(1024)}, u32[]{:S(2)}, u32[]{:S(2)}) collective-permute-start(f32[221184]{0:T(1024)} %bitcast_dynamic-update-slice_fusion.1), channel_id=1, source_target_pairs={{0,1},{1,0},{2,3},{3,2},{4,5},{5,4},{6,7},{7,6},{8,9},{9,8},{10,11... | collective-permute-start | bytes 2654216 | tf_op jit(solution)/shard_map/ppermute | solution.py:14
  498.7 21.5 %collective-permute-start.1 = (f32[221184]{0:T(1024)}, f32[221184]{0:T(1024)}, u32[]{:S(2)}, u32[]{:S(2)}) collective-permute-start(f32[221184]{0:T(1024)} %broadcast_select_fusion), channel_id=1, source_target_pairs={{0,2},{1,3},{2,0},{3,1},{4,6},{5,7},{6,4},{7,5},{8,10},{9,11},{10,... | collective-permute-start | bytes 2654216 | tf_op jit(solution)/shard_map/ppermute | solution.py:14
  522.5 46.4 %copy-start.15 = (s32[3]{0:T(128)S(1)}, s32[3]{0:T(128)}, u32[]{:S(2)}) copy-start(s32[3]{0:T(128)} %constant.237.clone.1) | copy-start | bytes 40
  522.5 47.2 %copy-start.9 = (f32[64,4,128]{2,0,1:T(8,128)S(1)}, f32[64,4,128]{2,0,1:T(8,128)}, u32[]{:S(2)}) copy-start(f32[64,4,128]{2,0,1:T(8,128)} %fusion.73) | copy-start | bytes 393220
  522.5 22.2 %collective-permute-start.2 = (f32[221184]{0:T(1024)}, f32[221184]{0:T(1024)}, u32[]{:S(2)}, u32[]{:S(2)}) collective-permute-start(f32[221184]{0:T(1024)} %broadcast_select_fusion.1), channel_id=1, source_target_pairs={{0,4},{1,5},{2,6},{3,7},{4,0},{5,1},{6,2},{7,3},{8,12},{9,13},{10,... | collective-permute-start | bytes 2654216 | tf_op jit(solution)/shard_map/ppermute | solution.py:14
  546.8 19.8 %collective-permute-start.3 = (f32[221184]{0:T(1024)}, f32[221184]{0:T(1024)}, u32[]{:S(2)}, u32[]{:S(2)}) collective-permute-start(f32[221184]{0:T(1024)} %broadcast_select_fusion.2), channel_id=1, source_target_pairs={{0,8},{1,9},{2,10},{3,11},{4,12},{5,13},{6,14},{7,15},{8,0},{9,1},... | collective-permute-start | bytes 2654216 | tf_op jit(solution)/shard_map/ppermute | solution.py:14
  546.8 48.7 %copy-start.13 = (s32[4,11,1]{1,0,2:T(4,128)S(1)}, s32[4,11,1]{1,0,2:T(4,128)}, u32[]{:S(2)}) copy-start(s32[4,11,1]{1,0,2:T(4,128)} %get-tuple-element.100) | copy-start | bytes 532
  568.9 20.5 %collective-permute-start.4 = (f32[221184]{0:T(1024)}, f32[221184]{0:T(1024)}, u32[]{:S(2)}, u32[]{:S(2)}) collective-permute-start(f32[221184]{0:T(1024)} %broadcast_select_fusion.3), channel_id=1, source_target_pairs={{0,16},{1,17},{2,18},{3,19},{4,20},{5,21},{6,22},{7,23},{8,24},{9,... | collective-permute-start | bytes 2654216 | tf_op jit(solution)/shard_map/ppermute | solution.py:14
  590.6 0.9 copy-start.7
  594.2 128.6 %reduce-scatter.5.cloned.1.call-start = ((), (), s32[]{:S(2)}) async-start(), calls=%async_computation.5 | async-start | bytes 4325376 | tf_op jit(solution)/shard_map/reduce_scatter | solution.py:42
  595.5 4.9 copy-start.5
  649.0 225.2 %copy-start.6 = (f32[4,64,128]{2,1,0:T(8,128)S(1)}, f32[4,64,128]{2,1,0:T(8,128)}, u32[]{:S(2)}) copy-start(f32[4,64,128]{2,1,0:T(8,128)} %get-tuple-element.97) | copy-start | bytes 393220
  649.0 226.1 %copy-start.11 = (f32[4,64,128]{2,1,0:T(8,128)S(1)}, f32[4,64,128]{2,1,0:T(8,128)}, u32[]{:S(2)}) copy-start(f32[4,64,128]{2,1,0:T(8,128)} %copy-done.10) | copy-start | bytes 393220
  (1 other events, 0.7 us)
Sparse Core Ops, SparseCore 0:
  10.3 49.7 all-gather.2
  63.7 79.6 reduce-scatter.2
  594.3 45.1 all-gather.4
  643.0 79.7 reduce-scatter.4
